TPU v7x, 128 devices: a whole 4x4x4 slice. The times are simulated.
128 devices in a mesh: dp: 8 (over z, core), expert: 16 (over y, x).
Axes of the slice: x: 4, y: 4, z: 4, core: 2. Of those that a mesh axis runs over, the one named last changes fastest.
Arguments:
- inputs: bfloat16 [16384, 2048], P(('dp', 'expert')), may hold values from -6 to 6
- out_grad: bfloat16 [16384, 2048], P(('dp', 'expert')), may hold values from -6 to 6
- combine: float32 [16384, 8], P(('dp', 'expert')), may hold values from 0 to 1, as said below
- routes: int32 [16384, 8], P(('dp', 'expert')), may hold values from 0 to 63, all different within a row; in each aligned block of 128 rows (0 to 127, 128 to 255, ...) at most 24 rows name the same one
- saved_hidden: bfloat16 [8, 64, 16, 24, 768], P('dp', 'expert'), may hold values from -6 to 6
- down_weight: bfloat16 [64, 2048, 768], P('expert'), may hold values from -0.21875 to 0.21875
- router_weight: bfloat16 [64, 2048], replicated, may hold values from -0.125 to 0.125
Outputs:
- hidden_grad: bfloat16 [8, 64, 16, 24, 768], P('dp', 'expert')
- down_grad: bfloat16 [64, 2048, 768], P('expert', 'dp')
- input_grad: bfloat16 [16384, 2048], P(('dp', 'expert'))
- router_grad: float32 [64, 2048], replicated
Inputs may be any that keep to these rules, and one draw needn't show every extreme that they name: `routes`: each token names 8 different experts; among the 128 tokens of one device no expert is named by more than 24 tokens, a bound that some block reaches. `combine`: each token's 8 weights are positive and sum to one.
All inputs are finite; a program needn't handle non-finite values.
Results may differ from a plain program's by a relative error of at most 0.017.
Values may be sent and summed in bfloat16 or wider, within the bound.
A program may use at most 128 MiB of HBM per device.

v0:
```python
import jax
import jax.numpy as jnp
from jax import lax
from jax.sharding import PartitionSpec as P


def make_marks(block_routes, total_experts):
    return block_routes[:, :, None] == jnp.arange(total_experts, dtype=jnp.int32)[None, None, :]


def slot_positions(route_marks):
    counts = jnp.sum(route_marks.astype(jnp.bfloat16), axis=1)
    token_order = jnp.arange(route_marks.shape[0], dtype=jnp.int32)
    earlier = (token_order[None, :] < token_order[:, None]).astype(jnp.bfloat16)
    before = jnp.dot(earlier, counts, preferred_element_type=jnp.float32)
    picked = jnp.sum(jnp.where(route_marks, before[:, None, :], 0.0), axis=2)
    return picked.astype(jnp.int32)


def pack_rows(scaled, lane_index, owner_slot, positions, local_experts, groups, capacity):
    width = scaled.shape[-1]
    flat_index = (owner_slot * groups + lane_index) * capacity + positions
    zero_rows = jnp.zeros((local_experts * groups * capacity, width), jnp.bfloat16)
    filled = zero_rows.at[flat_index.reshape(-1)].set(scaled.reshape(-1, width))
    return filled.reshape(local_experts, groups, capacity, width)


def local(inputs, out_grad, combine, routes, saved_hidden, down_weight, router_weight):
    token_count, width = out_grad.shape
    local_experts = down_weight.shape[0]
    total_experts = router_weight.shape[0]
    groups = lax.axis_size("expert")
    capacity = saved_hidden.shape[3]
    hidden_width = saved_hidden.shape[4]
    route_marks = make_marks(routes, total_experts)
    positions = slot_positions(route_marks)
    owner_dev = routes // local_experts
    owner_slot = routes % local_experts
    scaled = (combine[:, :, None] * out_grad[:, None, :].astype(jnp.float32)).astype(jnp.bfloat16)
    packed = pack_rows(scaled, owner_dev, owner_slot, positions, local_experts, groups, capacity)
    received = lax.all_to_all(packed, "expert", split_axis=1, concat_axis=1, tiled=True)
    hidden_local = saved_hidden[0]
    products_list = []
    hidden_list = []
    weight_terms = []
    for expert in range(local_experts):
        slot_rows = received[expert].reshape(groups * capacity, width)
        slot_acts = hidden_local[expert].reshape(groups * capacity, hidden_width)
        weight = down_weight[expert]
        recomputed = lax.dot_general(
            slot_acts, weight, (((1,), (1,)), ((), ())), preferred_element_type=jnp.float32
        )
        products_list.append(jnp.sum(recomputed * slot_rows.astype(jnp.float32), axis=1))
        hidden_list.append(
            jnp.dot(slot_rows, weight, preferred_element_type=jnp.float32).astype(jnp.bfloat16)
        )
        weight_terms.append(
            lax.dot_general(
                slot_rows, slot_acts, (((0,), (0,)), ((), ())), preferred_element_type=jnp.float32
            )
        )
    down_grad = lax.psum_scatter(
        jnp.stack(weight_terms).astype(jnp.bfloat16), "dp", scatter_dimension=1, tiled=True
    )
    hidden_grad = jnp.stack(hidden_list).reshape(1, local_experts, groups, capacity, hidden_width)
    slot_products = jnp.stack(products_list).reshape(local_experts, groups, capacity)
    returned = lax.all_to_all(slot_products, "expert", split_axis=1, concat_axis=1, tiled=True)
    pair_index = (owner_slot * groups + owner_dev) * capacity + positions
    pair_sums = returned.reshape(-1)[pair_index]
    logit_grad = pair_sums - combine * jnp.sum(pair_sums, axis=1, keepdims=True)
    dense_grad = jnp.sum(jnp.where(route_marks, logit_grad[:, :, None], 0.0), axis=1).astype(
        jnp.bfloat16
    )
    input_grad = jnp.dot(dense_grad, router_weight, preferred_element_type=jnp.float32).astype(
        jnp.bfloat16
    )
    router_part = lax.dot_general(
        dense_grad, inputs, (((0,), (0,)), ((), ())), preferred_element_type=jnp.float32
    )
    router_grad = lax.psum(router_part, ("dp", "expert"))
    return (hidden_grad, down_grad, input_grad, router_grad)


def solution(mesh):
    placed = (
        P(("dp", "expert"), None),
        P(("dp", "expert"), None),
        P(("dp", "expert"), None),
        P(("dp", "expert"), None),
        P("dp", "expert", None, None, None),
        P("expert", None, None),
        P(),
    )
    return jax.shard_map(
        local,
        mesh=mesh,
        in_specs=placed,
        out_specs=(
            P("dp", "expert", None, None, None),
            P("expert", "dp", None),
            P(("dp", "expert"), None),
            P(),
        ),
        check_vma=False,
    )
```

profile of v0, /device:TPU:1, one launch (start us, length us, event | category | flops | bytes accessed | tf_op | source)
XLA Modules:
  0.0 366.2 jit_solution(16921963926218966697)
XLA Ops:
  8.0 0.8 fusion.55
  8.8 0.1 fusion.56
  8.9 0.7 select_reduce_fusion.1
  9.7 0.7 compare_select_fusion.1
  10.4 0.1 copy.45
  10.5 0.1 reshape.82
  10.6 0.8 copy.46
  11.4 0.1 mul.48
  11.5 1.1 convert_element_type.50
  12.6 10.6 %scatter_custom_fusion = bf16[1536,2048]{1,0:T(8,128)(2,1)} fusion(s32[1024]{0:T(1024)S(1)} %bitcast.110, f32[128,2048]{1,0:T(8,128)S(1)} %convert_element_type.50, f32[1024]{0:T(1024)S(1)} %mul.48, bf16[]{:T(256)} %constant.31.clone.1), kind=kCustom, calls=%fused_computation.5 | custom fusion | flops 4194304 | bytes 7344130 | tf_op jit(solution)/shard_map/scatter | solution.py:24
  23.2 6.6 %copy.47 = bf16[4,16,24,2048]{3,2,0,1:T(8,128)(2,1)} copy(bf16[4,16,24,2048]{3,2,1,0:T(8,128)(2,1)} %bitcast.85) | data formatting | bytes 12582912 | tf_op jit(solution)/shard_map/reshape | solution.py:25
  29.8 7.8 %all-to-all-start = ((bf16[4,16,24,2048]{3,2,0,1:T(8,128)(2,1)}), bf16[4,16,24,2048]{3,2,0,1:T(8,128)(2,1)}, u32[]{:S(2)}, u32[]{:S(2)}) async-start(bf16[4,16,24,2048]{3,2,0,1:T(8,128)(2,1)} %copy.47), calls=%async_computation | async-start | bytes 12582912 | tf_op jit(solution)/shard_map/all_to_all | solution.py:41
  37.6 0.1 copy.49
  37.7 0.1 reshape.87
  37.8 1.2 fusion.70
  39.0 90.8 %all-to-all-done = bf16[4,16,24,2048]{3,2,0,1:T(8,128)(2,1)} async-done(((bf16[4,16,24,2048]{3,2,0,1:T(8,128)(2,1)}), bf16[4,16,24,2048]{3,2,0,1:T(8,128)(2,1)}, u32[]{:S(2)}, u32[]{:S(2)}) %all-to-all-start) | async-done | bytes 6291488 | tf_op jit(solution)/shard_map/all_to_all | solution.py:41
  129.9 4.8 %fusion.69 = (bf16[1,16,24,2048]{3,2,0,1:T(8,128)(2,1)S(1)}, bf16[1,16,24,2048]{3,2,0,1:T(8,128)(2,1)}, bf16[1,16,24,2048]{3,2,0,1:T(8,128)(2,1)S(1)}, bf16[1,16,24,2048]{3,2,0,1:T(8,128)(2,1)S(1)}) fusion(bf16[4,16,24,2048]{3,2,0,1:T(8,128)(2,1)} %all-to-all-done), kind=kLoop, calls=%fused_computation.80 | loop fusion | bytes 12582912 | tf_op jit(solution)/shard_map/slice | solution.py:47
  134.7 3.5 fusion.23
  138.2 3.6 multiply_reduce_fusion.2
  141.9 1.5 multiply_reduce_fusion.1
  143.4 3.5 fusion.24
  146.9 1.5 multiply_reduce_fusion.3
  148.4 3.5 fusion.22
  151.9 0.1 stack.61
  152.0 0.1 stack.62
  152.1 0.1 stack.60
  152.2 3.9 %multiply_reduce_fusion = f32[384]{0:T(512)S(1)} fusion(bf16[384,2048]{1,0:T(8,128)(2,1)} %bitcast.95, bf16[384,768]{1,0:T(8,128)(2,1)S(1)} %bitcast.98, bf16[4,2048,768]{2,1,0:T(8,128)(2,1)} %param.12), kind=kOutput, calls=%fused_computation.28 | convolution fusion | flops 1210318464 | bytes 5309952 | tf_op jit(solution)/shard_map/dot_general | solution.py:50
  156.1 0.1 stack.63
  156.2 0.7 pad_maximum_fusion.2
  156.9 5.4 %all-to-all-start.1 = ((f32[4,16,24]{2,0,1:T(4,128)}), f32[4,16,24]{2,0,1:T(4,128)S(1)}, u32[]{:S(2)}, u32[]{:S(2)}) async-start(f32[4,16,24]{2,0,1:T(4,128)} %pad_maximum_fusion.2), calls=%async_computation.2 | async-start | bytes 65536 | tf_op jit(solution)/shard_map/all_to_all | solution.py:67
  162.3 0.3 all-reduce.2.cloned.1.call-start
  162.6 4.9 %fusion.25 = bf16[1,2048,768]{2,1,0:T(8,128)(2,1)} fusion(bf16[384,2048]{1,0:T(8,128)(2,1)} %bitcast.96, bf16[384,768]{1,0:T(8,128)(2,1)S(1)} %bitcast.99), kind=kOutput, calls=%fused_computation.36 | convolution fusion | flops 1209532416 | bytes 5308416 | tf_op jit(solution)/shard_map/dot_general | solution.py:58
  167.5 1.3 all-to-all-done.1
  168.7 0.1 reshape.84
  168.8 6.2 %gather_fusion = f32[1024]{0:T(1024)S(1)} fusion(f32[1536]{0:T(1024)S(1)} %reshape.84, s32[1024]{0:T(1024)S(1)} %broadcast_clamp_fusion), kind=kCustom, calls=%fused_computation | custom fusion | bytes 12288 | tf_op jit(solution)/shard_map/gather | solution.py:69
  175.0 0.1 reshape.86
  175.1 0.1 reduce_sum.81
  175.4 1.0 fusion.71
  176.4 0.0 reduce-scatter.2.cloned.1.call-start
  176.5 10.7 %pad_maximum_fusion = bf16[4,2048,768]{2,1,0:T(8,128)(2,1)} fusion(bf16[1,2048,768]{2,1,0:T(8,128)(2,1)} %fusion.25, bf16[1,2048,768]{2,1,0:T(8,128)(2,1)} %fusion.24, bf16[1,2048,768]{2,1,0:T(8,128)(2,1)} %fusion.23, bf16[1,2048,768]{2,1,0:T(8,128)(2,1)} %fusion.22), kind=kLoop, calls=%fused_computation.2 | loop fusion | flops 18874368 | bytes 25165824 | tf_op jit(solution)/shard_map/stack | solution.py:63
  187.2 3.9 %fusion.51 = bf16[384,768]{1,0:T(8,128)(2,1)S(1)} fusion(bf16[384,2048]{1,0:T(8,128)(2,1)} %bitcast.97, bf16[4,2048,768]{2,1,0:T(8,128)(2,1)} %param.12), kind=kOutput, calls=%fused_computation.50 | convolution fusion | flops 1208254464 | bytes 5308416 | tf_op jit(solution)/shard_map/dot_general | solution.py:55
  191.1 3.4 fusion.42
  194.6 3.3 fusion.48
  197.9 4.1 %fusion.45 = bf16[384,768]{1,0:T(8,128)(2,1)S(1)} fusion(bf16[384,2048]{1,0:T(8,128)(2,1)S(1)} %bitcast.88, bf16[4,2048,768]{2,1,0:T(8,128)(2,1)} %param.12), kind=kOutput, calls=%fused_computation.48 | convolution fusion | flops 1208254464 | bytes 5308416 | tf_op jit(solution)/shard_map/dot_general | solution.py:55
  202.0 1.7 pad_maximum_fusion.1
  203.7 1.1 convolution_convert_fusion.4
  204.9 152.0 %all-reduce.2.cloned.1.call-done = f32[64,2048]{1,0:T(8,128)} async-done(((f32[64,2048]{1,0:T(8,128)}), f32[64,2048]{1,0:T(8,128)}) %all-reduce.2.cloned.1.call-update) | async-done | bytes 524304 | tf_op jit(solution)/shard_map/psum | solution.py:80
  356.9 1.9 copy.52
  (40 shorter events, 0.2 us)
Async XLA Ops:
  8.0 167.4 %copy-start = (bf16[128,2048]{1,0:T(8,128)(2,1)S(1)}, bf16[128,2048]{1,0:T(8,128)(2,1)}, u32[]{:S(2)}) copy-start(bf16[128,2048]{1,0:T(8,128)(2,1)} %param.7) | copy-start | bytes 1572868
  29.8 8.0 %copy-start.1 = (bf16[1,4,16,24,768]{4,3,2,1,0:T(8,128)(2,1)S(1)}, bf16[1,4,16,24,768]{4,3,2,1,0:T(8,128)(2,1)}, u32[]{:S(2)}) copy-start(bf16[1,4,16,24,768]{4,3,2,1,0:T(8,128)(2,1)} %param.11) | copy-start | bytes 7077892
  29.8 100.1 %all-to-all-start = ((bf16[4,16,24,2048]{3,2,0,1:T(8,128)(2,1)}), bf16[4,16,24,2048]{3,2,0,1:T(8,128)(2,1)}, u32[]{:S(2)}, u32[]{:S(2)}) async-start(bf16[4,16,24,2048]{3,2,0,1:T(8,128)(2,1)} %copy.47), calls=%async_computation | async-start | bytes 12582912 | tf_op jit(solution)/shard_map/all_to_all | solution.py:41
  39.0 95.7 %copy-start.8 = (bf16[1,1,16,24,768]{4,3,2,1,0:T(8,128)(2,1)S(1)}, bf16[1,1,16,24,768]{4,3,2,1,0:T(8,128)(2,1)}, u32[]{:S(2)}) copy-start(bf16[1,1,16,24,768]{4,3,2,1,0:T(8,128)(2,1)} %get-tuple-element.11) | copy-start | bytes 1769476
  129.9 11.9 %slice-start = ((s8[12582912]{0:T(1024)(128)(4,1)}), s8[4194304]{0:T(1024)(128)(4,1)S(1)}, s32[]{:S(2)}) async-start(s8[12582912]{0:T(1024)(128)(4,1)} %bitcast.111), calls=%async_computation.5 | async-start | bytes 8388608
  129.9 11.9 %slice-start.1 = ((s8[12582912]{0:T(1024)(128)(4,1)}), s8[4194304]{0:T(1024)(128)(4,1)S(1)}, s32[]{:S(2)}) async-start(s8[12582912]{0:T(1024)(128)(4,1)} %bitcast.111), calls=%async_computation.6 | async-start | bytes 8388608
  134.7 8.7 %copy-start.2 = (bf16[1,16,24,2048]{3,2,0,1:T(8,128)(2,1)}, bf16[1,16,24,2048]{3,2,0,1:T(8,128)(2,1)S(1)}, u32[]{:S(2)}) copy-start(bf16[1,16,24,2048]{3,2,0,1:T(8,128)(2,1)S(1)} %get-tuple-element.8) | copy-start | bytes 4718596
  134.7 13.7 %copy-start.4 = (bf16[1,16,24,2048]{3,2,0,1:T(8,128)(2,1)}, bf16[1,16,24,2048]{3,2,0,1:T(8,128)(2,1)S(1)}, u32[]{:S(2)}) copy-start(bf16[1,16,24,2048]{3,2,0,1:T(8,128)(2,1)S(1)} %get-tuple-element.6) | copy-start | bytes 4718596
  138.2 3.6 copy-start.7
  138.2 3.6 slice-start.2
  143.4 3.5 copy-start.6
  156.9 11.8 %all-to-all-start.1 = ((f32[4,16,24]{2,0,1:T(4,128)}), f32[4,16,24]{2,0,1:T(4,128)S(1)}, u32[]{:S(2)}, u32[]{:S(2)}) async-start(f32[4,16,24]{2,0,1:T(4,128)} %pad_maximum_fusion.2), calls=%async_computation.2 | async-start | bytes 65536 | tf_op jit(solution)/shard_map/all_to_all | solution.py:67
  162.3 194.6 %all-reduce.2.cloned.1.call-start = ((), (), s32[]{:S(2)}) async-start(), calls=%async_computation.4 | async-start | bytes 1048576 | tf_op jit(solution)/shard_map/psum | solution.py:80
  168.8 6.5 %copy-start.11 = (f32[128,8]{0,1:T(8,128)S(1)}, f32[128,8]{0,1:T(8,128)}, u32[]{:S(2)}) copy-start(f32[128,8]{0,1:T(8,128)} %param.9) | copy-start | bytes 12292
  168.8 6.5 %copy-start.10 = (s32[128,8]{0,1:T(8,128)S(1)}, s32[128,8]{0,1:T(8,128)}, u32[]{:S(2)}) copy-start(s32[128,8]{0,1:T(8,128)} %param.10) | copy-start | bytes 12292
  176.4 180.5 %reduce-scatter.2.cloned.1.call-start = ((), (), s32[]{:S(2)}) async-start(), calls=%async_computation.3 | async-start | bytes 14155776 | tf_op jit(solution)/shard_map/reduce_scatter | solution.py:62
  187.2 3.9 %copy-start.5 = (bf16[1,16,24,2048]{3,2,0,1:T(8,128)(2,1)S(1)}, bf16[1,16,24,2048]{3,2,0,1:T(8,128)(2,1)}, u32[]{:S(2)}) copy-start(bf16[1,16,24,2048]{3,2,0,1:T(8,128)(2,1)} %copy-done.4) | copy-start | bytes 4718596
  191.1 3.5 copy-start.3
  202.0 1.7 copy-start.9
Sparse Core Ops, SparseCore 0:
  176.5 180.2 all-reduce.1
Sparse Core Ops, SparseCore 1:
  187.3 75.3 reduce-scatter.1
where the time goes:
time: 367 us; the launch traced here: 366 us
  waiting for transfers between devices  244 us (66%)
  matrix products  43 us (12%)
  other arithmetic  27.2 us (7%)
  local copies, waits for them, and re-layouts  22.6 us (6%)
  between operations  15.8 us (4%)
  starting transfers between devices  13.5 us (4%)
    psum x1, waiting for transfers between devices, local(): router_grad = lax.psum(router_part, ('dp', 'expert'))  152 us
    all_to_all x1, waiting for transfers between devices, local(): lax.all_to_all(packed, 'expert', split_axis=1, concat_axis=1, tiled=True)  90.8 us
    dot_general x4, matrix products, local(): lax.dot_general(slot_rows, slot_acts, (((0,), (0,)), ((), ())), preferred...  15.5 us
    dot_general x4, matrix products, local(): jnp.dot(slot_rows, weight, preferred_element_type=jnp.float32)  14.8 us
    another operation x1, other arithmetic, local(): jnp.stack(weight_terms).astype(jnp.bfloat16)  10.7 us
    scatter x1, other arithmetic, pack_rows(): filled = zero_rows.at[flat_index.reshape(-1)].set(scaled.reshape(-1, width))  10.6 us
    dot_general x4, matrix products, local(): lax.dot_general(slot_acts, weight, (((1,), (1,)), ((), ())), preferred_el...  10.5 us
    all_to_all x1, starting transfers between devices, local(): lax.all_to_all(packed, 'expert', split_axis=1, concat_axis=1, tiled=True)  7.77 us
  transfers between devices with their start and end apart: 4, of which 3 were waited for; matrix products, arithmetic and copies ran while one was open for 9% of the time, Pallas kernels for 0%

commit v1 on v0

--- a/solution.py
+++ b/solution.py
@@ -77,7 +77,9 @@
     router_part = lax.dot_general(
         dense_grad, inputs, (((0,), (0,)), ((), ())), preferred_element_type=jnp.float32
     )
-    router_grad = lax.psum(router_part, ("dp", "expert"))
+    router_grad = router_part
+    for mesh_axis in ("dp", "expert"):
+        router_grad = lax.psum(router_grad, mesh_axis)
     return (hidden_grad, down_grad, input_grad, router_grad)
 
 

time: 367 us -> 411 us (1.12)
  waiting for transfers between devices: 244 us -> 285 us
  matrix products: 43 us -> 47.8 us
    reduce_scatter x1, waiting for transfers between devices: 0.01 us -> 75.6 us  [local(): lax.psum_scatter(jnp.stack(weight_terms).astype(jnp.bfloat16), 'dp', scat...]
    psum x1 -> x2, waiting for transfers between devices: 152 us -> 117 us  [local(): router_grad = lax.psum(router_grad, mesh_axis)]
    dot_general x4, matrix products: 10.5 us -> 14.7 us  [local(): lax.dot_general(slot_acts, weight, (((1,), (1,)), ((), ())), preferred_el...]
  transfers between devices with their start and end apart: 4 -> 5, of which waited for: 3 -> 5; matrix products, arithmetic and copies ran while one was open for 9% -> 9% of each run, Pallas kernels for 0% -> 0%
where the time goes in v1:
time: 411 us
  waiting for transfers between devices  285 us (69%)
  matrix products  47.8 us (12%)
  other arithmetic  27.2 us (7%)
  local copies, waits for them, and re-layouts  23.2 us (6%)
  between operations  14 us (3%)
  starting transfers between devices  13.5 us (3%)
    psum x2, waiting for transfers between devices, local(): router_grad = lax.psum(router_grad, mesh_axis)  117 us
    all_to_all x1, waiting for transfers between devices, local(): lax.all_to_all(packed, 'expert', split_axis=1, concat_axis=1, tiled=True)  90.8 us
    reduce_scatter x1, waiting for transfers between devices, local(): lax.psum_scatter(jnp.stack(weight_terms).astype(jnp.bfloat16), 'dp', scat...  75.6 us
    dot_general x4, matrix products, local(): lax.dot_general(slot_rows, slot_acts, (((0,), (0,)), ((), ())), preferred...  16.9 us
    dot_general x4, matrix products, local(): lax.dot_general(slot_acts, weight, (((1,), (1,)), ((), ())), preferred_el...  14.7 us
    dot_general x4, matrix products, local(): jnp.dot(slot_rows, weight, preferred_element_type=jnp.float32)  14 us
    another operation x1, other arithmetic, local(): jnp.stack(weight_terms).astype(jnp.bfloat16)  10.7 us
    scatter x1, other arithmetic, pack_rows(): filled = zero_rows.at[flat_index.reshape(-1)].set(scaled.reshape(-1, width))  10.6 us
  transfers between devices with their start and end apart: 5, of which 5 were waited for; matrix products, arithmetic and copies ran while one was open for 9% of the time, Pallas kernels for 0%

profile of v1, /device:TPU:1, one launch (start us, length us, event | category | flops | bytes accessed | tf_op | source)
XLA Modules:
  0.0 410.6 jit_solution(15486615265287168678)
XLA Ops:
  7.2 0.8 fusion.55
  8.0 0.1 fusion.56
  8.1 0.7 select_reduce_fusion.1
  8.8 0.7 compare_select_fusion.1
  9.6 0.1 copy.45
  9.7 0.1 reshape.82
  9.8 0.8 copy.46
  10.6 0.1 mul.48
  10.6 1.1 convert_element_type.50
  11.8 10.6 %scatter_custom_fusion = bf16[1536,2048]{1,0:T(8,128)(2,1)} fusion(s32[1024]{0:T(1024)S(1)} %bitcast.110, f32[128,2048]{1,0:T(8,128)S(1)} %convert_element_type.50, f32[1024]{0:T(1024)S(1)} %mul.48, bf16[]{:T(256)} %constant.31.clone.1), kind=kCustom, calls=%fused_computation.5 | custom fusion | flops 4194304 | bytes 7344130 | tf_op jit(solution)/shard_map/scatter | solution.py:24
  22.4 6.6 %copy.47 = bf16[4,16,24,2048]{3,2,0,1:T(8,128)(2,1)} copy(bf16[4,16,24,2048]{3,2,1,0:T(8,128)(2,1)} %bitcast.85) | data formatting | bytes 12582912 | tf_op jit(solution)/shard_map/reshape | solution.py:25
  29.0 7.8 %all-to-all-start = ((bf16[4,16,24,2048]{3,2,0,1:T(8,128)(2,1)}), bf16[4,16,24,2048]{3,2,0,1:T(8,128)(2,1)}, u32[]{:S(2)}, u32[]{:S(2)}) async-start(bf16[4,16,24,2048]{3,2,0,1:T(8,128)(2,1)} %copy.47), calls=%async_computation | async-start | bytes 12582912 | tf_op jit(solution)/shard_map/all_to_all | solution.py:41
  36.7 0.1 copy.49
  36.8 0.1 reshape.87
  37.0 1.2 fusion.70
  38.2 90.8 %all-to-all-done = bf16[4,16,24,2048]{3,2,0,1:T(8,128)(2,1)} async-done(((bf16[4,16,24,2048]{3,2,0,1:T(8,128)(2,1)}), bf16[4,16,24,2048]{3,2,0,1:T(8,128)(2,1)}, u32[]{:S(2)}, u32[]{:S(2)}) %all-to-all-start) | async-done | bytes 6291488 | tf_op jit(solution)/shard_map/all_to_all | solution.py:41
  129.0 5.4 %fusion.69 = (bf16[1,16,24,2048]{3,2,0,1:T(8,128)(2,1)}, bf16[1,16,24,2048]{3,2,0,1:T(8,128)(2,1)}, bf16[1,16,24,2048]{3,2,0,1:T(8,128)(2,1)S(1)}, bf16[1,16,24,2048]{3,2,0,1:T(8,128)(2,1)S(1)}) fusion(bf16[4,16,24,2048]{3,2,0,1:T(8,128)(2,1)} %all-to-all-done), kind=kLoop, calls=%fused_computation.80 | loop fusion | bytes 12582912 | tf_op jit(solution)/shard_map/slice | solution.py:47
  134.5 3.5 fusion.23
  138.0 3.5 multiply_reduce_fusion.2
  141.5 3.4 multiply_reduce_fusion.1
  144.9 3.5 fusion.24
  148.4 0.1 stack.61
  148.5 0.1 stack.62
  148.6 3.9 multiply_reduce_fusion.3
  152.5 0.1 stack.60
  152.6 3.9 multiply_reduce_fusion
  156.5 0.1 stack.63
  156.6 0.7 pad_maximum_fusion.2
  157.3 5.4 %all-to-all-start.1 = ((f32[4,16,24]{2,0,1:T(4,128)}), f32[4,16,24]{2,0,1:T(4,128)S(1)}, u32[]{:S(2)}, u32[]{:S(2)}) async-start(f32[4,16,24]{2,0,1:T(4,128)} %pad_maximum_fusion.2), calls=%async_computation.2 | async-start | bytes 65536 | tf_op jit(solution)/shard_map/all_to_all | solution.py:67
  162.7 5.0 %fusion.22 = bf16[1,2048,768]{2,1,0:T(8,128)(2,1)} fusion(bf16[384,2048]{1,0:T(8,128)(2,1)} %bitcast.93, bf16[384,768]{1,0:T(8,128)(2,1)S(1)} %bitcast.101), kind=kOutput, calls=%fused_computation.33 | convolution fusion | flops 1209532416 | bytes 5308416 | tf_op jit(solution)/shard_map/dot_general | solution.py:58
  167.7 1.4 all-to-all-done.1
  169.2 0.1 reshape.84
  169.3 6.2 %gather_fusion = f32[1024]{0:T(1024)S(1)} fusion(f32[1536]{0:T(1024)S(1)} %reshape.84, s32[1024]{0:T(1024)S(1)} %broadcast_clamp_fusion), kind=kCustom, calls=%fused_computation | custom fusion | bytes 12288 | tf_op jit(solution)/shard_map/gather | solution.py:69
  175.6 0.1 reduce_sum.81
  175.8 1.0 fusion.71
  176.8 0.3 all-reduce.5.cloned.1.call-start
  177.1 4.9 %fusion.25 = bf16[1,2048,768]{2,1,0:T(8,128)(2,1)} fusion(bf16[384,2048]{1,0:T(8,128)(2,1)} %bitcast.96, bf16[384,768]{1,0:T(8,128)(2,1)S(1)} %bitcast.99), kind=kOutput, calls=%fused_computation.36 | convolution fusion | flops 1209532416 | bytes 5308416 | tf_op jit(solution)/shard_map/dot_general | solution.py:58
  182.0 56.4 %all-reduce.3.cloned.1.call-done = f32[64,2048]{1,0:T(8,128)} async-done(((f32[64,2048]{1,0:T(8,128)}), f32[64,2048]{1,0:T(8,128)}) %all-reduce.3.cloned.1.call-update) | async-done | bytes 524304 | tf_op jit(solution)/shard_map/psum | solution.py:82
  238.4 10.7 %pad_maximum_fusion = bf16[4,2048,768]{2,1,0:T(8,128)(2,1)} fusion(bf16[1,2048,768]{2,1,0:T(8,128)(2,1)} %fusion.25, bf16[1,2048,768]{2,1,0:T(8,128)(2,1)} %fusion.24, bf16[1,2048,768]{2,1,0:T(8,128)(2,1)} %fusion.23, bf16[1,2048,768]{2,1,0:T(8,128)(2,1)} %fusion.22), kind=kLoop, calls=%fused_computation.2 | loop fusion | flops 18874368 | bytes 25165824 | tf_op jit(solution)/shard_map/stack | solution.py:63
  249.2 3.9 fusion.51
  253.1 3.4 fusion.42
  256.6 3.3 fusion.48
  259.9 3.3 fusion.45
  263.2 1.7 pad_maximum_fusion.1
  264.9 1.1 convolution_convert_fusion.4
  266.0 60.6 %all-reduce.5.cloned.1.call-done = f32[64,2048]{1,0:T(8,128)} async-done(((f32[64,2048]{1,0:T(8,128)}), f32[64,2048]{1,0:T(8,128)}) %all-reduce.5.cloned.1.call-update) | async-done | bytes 524304 | tf_op jit(solution)/shard_map/psum | solution.py:82
  326.6 75.6 %reduce-scatter.2.cloned.1.call-done = bf16[4,256,768]{2,1,0:T(8,128)(2,1)} async-done(((bf16[4,2048,768]{2,1,0:T(8,128)(2,1)}), bf16[4,256,768]{2,1,0:T(8,128)(2,1)}) %reduce-scatter.2.cloned.1.call-update) | async-done | bytes 1572880 | tf_op jit(solution)/shard_map/reduce_scatter | solution.py:62
  402.2 1.9 copy.53
  (34 shorter events, 0.4 us)
Async XLA Ops:
  7.2 168.6 %copy-start = (bf16[128,2048]{1,0:T(8,128)(2,1)S(1)}, bf16[128,2048]{1,0:T(8,128)(2,1)}, u32[]{:S(2)}) copy-start(bf16[128,2048]{1,0:T(8,128)(2,1)} %param.7) | copy-start | bytes 1572868
  29.0 8.0 %copy-start.1 = (bf16[1,4,16,24,768]{4,3,2,1,0:T(8,128)(2,1)S(1)}, bf16[1,4,16,24,768]{4,3,2,1,0:T(8,128)(2,1)}, u32[]{:S(2)}) copy-start(bf16[1,4,16,24,768]{4,3,2,1,0:T(8,128)(2,1)} %param.11) | copy-start | bytes 7077892
  29.0 100.1 %all-to-all-start = ((bf16[4,16,24,2048]{3,2,0,1:T(8,128)(2,1)}), bf16[4,16,24,2048]{3,2,0,1:T(8,128)(2,1)}, u32[]{:S(2)}, u32[]{:S(2)}) async-start(bf16[4,16,24,2048]{3,2,0,1:T(8,128)(2,1)} %copy.47), calls=%async_computation | async-start | bytes 12582912 | tf_op jit(solution)/shard_map/all_to_all | solution.py:41
  38.2 96.3 %copy-start.7 = (bf16[1,1,16,24,768]{4,3,2,1,0:T(8,128)(2,1)S(1)}, bf16[1,1,16,24,768]{4,3,2,1,0:T(8,128)(2,1)}, u32[]{:S(2)}) copy-start(bf16[1,1,16,24,768]{4,3,2,1,0:T(8,128)(2,1)} %get-tuple-element.11) | copy-start | bytes 1769476
  134.5 10.4 %copy-start.2 = (bf16[1,16,24,2048]{3,2,0,1:T(8,128)(2,1)}, bf16[1,16,24,2048]{3,2,0,1:T(8,128)(2,1)S(1)}, u32[]{:S(2)}) copy-start(bf16[1,16,24,2048]{3,2,0,1:T(8,128)(2,1)S(1)} %get-tuple-element.8) | copy-start | bytes 4718596
  138.0 3.5 copy-start.6
  144.9 3.7 copy-start.5
  157.3 11.9 %all-to-all-start.1 = ((f32[4,16,24]{2,0,1:T(4,128)}), f32[4,16,24]{2,0,1:T(4,128)S(1)}, u32[]{:S(2)}, u32[]{:S(2)}) async-start(f32[4,16,24]{2,0,1:T(4,128)} %pad_maximum_fusion.2), calls=%async_computation.2 | async-start | bytes 65536 | tf_op jit(solution)/shard_map/all_to_all | solution.py:67
  162.7 75.7 %all-reduce.3.cloned.1.call-start = ((), (), s32[]{:S(2)}) async-start(), calls=%async_computation.4 | async-start | bytes 1048576 | tf_op jit(solution)/shard_map/psum | solution.py:82
  169.2 6.5 %copy-start.10 = (f32[128,8]{0,1:T(8,128)S(1)}, f32[128,8]{0,1:T(8,128)}, u32[]{:S(2)}) copy-start(f32[128,8]{0,1:T(8,128)} %param.9) | copy-start | bytes 12292
  169.3 6.5 %copy-start.9 = (s32[128,8]{0,1:T(8,128)S(1)}, s32[128,8]{0,1:T(8,128)}, u32[]{:S(2)}) copy-start(s32[128,8]{0,1:T(8,128)} %param.10) | copy-start | bytes 12292
  176.8 149.8 %all-reduce.5.cloned.1.call-start = ((), (), s32[]{:S(2)}) async-start(), calls=%async_computation.5 | async-start | bytes 1048576 | tf_op jit(solution)/shard_map/psum | solution.py:82
  238.4 163.9 %reduce-scatter.2.cloned.1.call-start = ((), (), s32[]{:S(2)}) async-start(), calls=%async_computation.3 | async-start | bytes 14155776 | tf_op jit(solution)/shard_map/reduce_scatter | solution.py:62
  249.2 4.0 copy-start.4
  253.1 3.4 copy-start.3
  263.2 1.7 copy-start.8
Sparse Core Ops, SparseCore 0:
  176.9 61.3 all-reduce.2
  241.9 84.6 all-reduce.4
  329.6 72.5 reduce-scatter.1
